TPU v7x, 32 devices: a whole 2x2x4 slice. The times are simulated.
32 devices in a mesh: tile: 8 (over y, x, core), col: 4 (over z).
Axes of the slice: x: 2, y: 2, z: 4, core: 2. Of those that a mesh axis runs over, the one named last changes fastest.
Arguments:
- impedance: bfloat16 [2, 16384, 16384], P(None, 'tile', 'col'), may hold values from -0.0234375 to 0.0234375
- mobility: bfloat16 [256, 64, 128], P('tile'), may hold values from -0.5 to 0.5
- force: bfloat16 [512, 256, 128], P('col', 'tile'), may hold values from -6 to 6
- patch_map: int32 [16384], replicated, may hold values from 0 to 16383, each once
- ownership: int32 [256], P('tile'), may hold values from 0 to 255, each once
Outputs:
- velocity: bfloat16 [512, 256, 128], P('col', 'tile')
- pressure: bfloat16 [512, 2, 16384], P('col', None, 'tile')
Inputs may be any that keep to these rules, and one draw needn't show every extreme that they name: `patch_map`: each patch appears exactly once. `ownership`: each panel appears exactly once.
All inputs are finite; a program needn't handle non-finite values.
Results may differ from a plain program's by a relative error of at most 0.018.
Values may be sent and summed in bfloat16 or wider, within the bound.
A program may use at most 128 MiB of HBM per device.

v0:
```python
import jax
import jax.numpy as jnp
from jax import lax
from jax.sharding import PartitionSpec as P

ITERS = 2


def per_device(impedance, mobility, force, patch_map, ownership):
    imp_re = impedance[0]
    imp_im = impedance[1]
    panel_width = mobility.shape[1]
    slot_count = mobility.shape[0]
    patch_count = patch_map.shape[0]
    loads_dev = force.shape[0]
    col_tiles = lax.axis_size("col")
    col_width = patch_count // col_tiles
    row_width = imp_re.shape[0]
    slot_flat = patch_map.reshape(-1, panel_width)[ownership].reshape(slot_count * panel_width)
    mob_re_t = jnp.transpose(mobility[:, :, :panel_width], (0, 2, 1))
    mob_im_t = jnp.transpose(mobility[:, :, panel_width:], (0, 2, 1))
    upper_rows = jnp.concatenate([mob_re_t, mob_im_t], 2)
    lower_rows = jnp.concatenate([-mob_im_t, mob_re_t], 2)
    real_form = jnp.concatenate([upper_rows, lower_rows], 1)

    def panel_response(drive):
        return jnp.einsum(
            "lsk,skj->lsj", drive, real_form, preferred_element_type=jnp.float32
        ).astype(jnp.bfloat16)

    velocity = panel_response(force)
    pressure = jnp.zeros((loads_dev, 2, row_width), jnp.bfloat16)
    for iteration in range(ITERS):
        values = (
            velocity.reshape(loads_dev, slot_count, 2, panel_width)
            .transpose(0, 2, 1, 3)
            .reshape(loads_dev, 2 * slot_count * panel_width)
        )
        base_pos = slot_flat // col_width * (2 * col_width) + slot_flat % col_width
        flat_index = jnp.concatenate([base_pos, base_pos + col_width])
        placed = jnp.zeros((loads_dev, 2 * patch_count), jnp.bfloat16).at[:, flat_index].set(values)
        placed = placed.reshape(loads_dev, col_tiles, 2, col_width)
        shares = lax.psum_scatter(
            placed.astype(jnp.float32).astype(jnp.bfloat16), "tile", scatter_dimension=3, tiled=True
        )
        moved = lax.all_to_all(shares, "col", split_axis=1, concat_axis=0, tiled=True)
        full_cols = lax.all_gather(moved, "tile", axis=3, tiled=True)
        columns = full_cols.reshape(full_cols.shape[0], 2 * col_width)
        vel_re = columns[:, :col_width]
        vel_im = columns[:, col_width:]
        contract = (((1,), (1,)), ((), ()))

        def dot_rows(left, right):
            return lax.dot_general(left, right, contract, preferred_element_type=jnp.float32)

        real_part = dot_rows(vel_re, imp_re) - dot_rows(vel_im, imp_im)
        imag_part = dot_rows(vel_re, imp_im) + dot_rows(vel_im, imp_re)
        summed = lax.psum_scatter(
            jnp.concatenate([real_part, imag_part], 1).astype(jnp.bfloat16),
            "col",
            scatter_dimension=0,
            tiled=True,
        )
        pressure = summed.reshape(loads_dev, 2, row_width)
        gathered = lax.all_gather(pressure, "tile", axis=2, tiled=True)
        picked = (
            gathered[:, :, slot_flat]
            .reshape(loads_dev, 2, slot_count, panel_width)
            .transpose(0, 2, 1, 3)
            .reshape(loads_dev, slot_count, 2 * panel_width)
        )
        drive = (force.astype(jnp.float32) - picked.astype(jnp.float32)).astype(jnp.bfloat16)
        velocity = panel_response(drive)
    return (velocity, pressure)


def solution(mesh):
    return jax.shard_map(
        per_device,
        mesh=mesh,
        in_specs=(
            P(None, "tile", "col"),
            P("tile", None, None),
            P("col", "tile", None),
            P(),
            P("tile"),
        ),
        out_specs=(P("col", "tile", None), P("col", None, "tile")),
        check_vma=False,
    )
```

profile of v0, /device:TPU:0, one launch (start us, length us, event | category | flops | bytes accessed | tf_op | source)
XLA Modules:
  0.0 846.8 jit_solution(14066625259313548850)
XLA Ops:
  8.6 2.4 slice_bitcast_fusion
  16.3 15.8 %scatter_custom_fusion = bf16[128,32768]{0,1:T(8,128)(2,1)} fusion(s32[4096]{0:T(1024)S(1)} %bitcast.108, bf16[4096,128]{1,0:T(8,128)(2,1)S(1)} %bitcast.101, bf16[]{:T(256)} %constant.36.clone.1), kind=kCustom, calls=%fused_computation.37 | custom fusion | bytes 8388610 | tf_op jit(solution)/shard_map/scatter | solution.py:41
  32.1 11.6 %copy.50 = bf16[128,4,2,4096]{3,0,2,1:T(8,128)(2,1)} copy(bf16[128,4,2,4096]{0,3,2,1:T(8,128)(2,1)} %bitcast.88) | data formatting | bytes 16777216 | tf_op jit(solution)/shard_map/reshape | solution.py:42
  43.8 74.1 %reduce-scatter.5.cloned.1.call-done = bf16[128,4,2,512]{3,0,2,1:T(8,128)(2,1)} async-done(((bf16[128,4,2,4096]{3,0,2,1:T(8,128)(2,1)}), bf16[128,4,2,512]{3,0,2,1:T(8,128)(2,1)}) %reduce-scatter.5.cloned.1.call-update) | async-done | bytes 1048592 | tf_op jit(solution)/shard_map/reduce_scatter | solution.py:43
  117.9 30.1 %all_to_all.36 = bf16[128,4,2,512]{3,0,2,1:T(8,128)(2,1)S(1)} all-to-all(bf16[128,4,2,512]{3,0,2,1:T(8,128)(2,1)} %reduce-scatter.5.cloned.1.call-done), channel_id=1, replica_groups=mesh['tile'=8,'col'=4] {'col'}, dimensions={1} | all-to-all | bytes 2097152 | tf_op jit(solution)/shard_map/all_to_all | solution.py:46
  149.4 53.9 %all-gather.5.cloned.1.call-done = bf16[512,1,2,4096]{3,0,2,1:T(8,128)(2,1)} async-done(((bf16[512,1,2,512]{3,0,2,1:T(8,128)(2,1)}), bf16[512,1,2,4096]{3,0,2,1:T(8,128)(2,1)}) %all-gather.5.cloned.1.call-update) | async-done | bytes 8388624 | tf_op jit(solution)/shard_map/all_gather | solution.py:47
  203.3 12.0 %copy.52 = bf16[512,1,2,4096]{0,3,2,1:T(8,128)(2,1)} copy(bf16[512,1,2,4096]{3,0,2,1:T(8,128)(2,1)} %all-gather.5.cloned.1.call-done) | data formatting | bytes 16777216 | tf_op jit(solution)/shard_map/all_gather | solution.py:47
  215.3 17.2 %fusion.4 = f32[512,2048]{1,0:T(8,128)} fusion(bf16[2,2048,4096]{2,1,0:T(8,128)(2,1)} %param.5, bf16[512,8192]{0,1:T(8,128)(2,1)} %bitcast.89), kind=kOutput, calls=%fused_computation.9 | convolution fusion | flops 8589934592 | bytes 25165824 | tf_op jit(solution)/shard_map/dot_general | solution.py:54
  232.5 14.1 %fusion.6 = f32[512,2048]{1,0:T(8,128)} fusion(bf16[2,2048,4096]{2,1,0:T(8,128)(2,1)} %param.5, bf16[512,8192]{0,1:T(8,128)(2,1)S(1)} %bitcast.92), kind=kOutput, calls=%fused_computation.11 | convolution fusion | flops 8589934592 | bytes 25165824 | tf_op jit(solution)/shard_map/dot_general | solution.py:54
  246.6 14.7 %add_convert_fusion.1 = bf16[512,2048]{1,0:T(8,128)(2,1)S(1)} fusion(f32[512,2048]{1,0:T(8,128)} %fusion.4, bf16[2,2048,4096]{2,1,0:T(8,128)(2,1)} %param.5, bf16[512,8192]{0,1:T(8,128)(2,1)} %bitcast.90), kind=kOutput, calls=%fused_computation.33 | convolution fusion | flops 8592031744 | bytes 27262976 | tf_op jit(solution)/shard_map/dot_general | solution.py:54
  261.3 14.3 %subtract_convert_fusion.1 = bf16[512,2048]{1,0:T(8,128)(2,1)S(1)} fusion(f32[512,2048]{1,0:T(8,128)} %fusion.6, bf16[2,2048,4096]{2,1,0:T(8,128)(2,1)} %param.5, bf16[512,8192]{0,1:T(8,128)(2,1)} %bitcast.91), kind=kOutput, calls=%fused_computation.34 | convolution fusion | flops 8592031744 | bytes 27262976 | tf_op jit(solution)/shard_map/dot_general | solution.py:54
  275.7 2.2 pad_maximum_fusion
  278.0 76.9 %reduce-scatter.7.cloned.1.call-done = bf16[128,4096]{1,0:T(8,128)(2,1)} async-done(((bf16[512,4096]{1,0:T(8,128)(2,1)}), bf16[128,4096]{1,0:T(8,128)(2,1)}) %reduce-scatter.7.cloned.1.call-update) | async-done | bytes 1048592 | tf_op jit(solution)/shard_map/reduce_scatter | solution.py:58
  356.7 3.1 copy.53
  359.9 54.8 %all-gather.7.cloned.1.call-done = bf16[128,2,16384]{0,1,2:T(2,128)(2,1)} async-done(((bf16[128,2,2048]{0,1,2:T(2,128)(2,1)}), bf16[128,2,16384]{0,1,2:T(2,128)(2,1)}) %all-gather.7.cloned.1.call-update) | async-done | bytes 8388624 | tf_op jit(solution)/shard_map/all_gather | solution.py:65
  414.7 10.6 %gather_fusion.1 = bf16[2048,128,2]{1,2,0:T(2,128)(2,1)S(1)} fusion(bf16[128,2,16384]{0,1,2:T(2,128)(2,1)} %all-gather.7.cloned.1.call-done, s32[2048]{0:T(1024)S(1)} %broadcast_clamp_fusion), kind=kCustom, calls=%fused_computation.1 | custom fusion | bytes 2105344 | tf_op jit(solution)/shard_map/gather | solution.py:67
  428.4 15.8 %scatter_custom_fusion.1 = bf16[128,32768]{0,1:T(8,128)(2,1)} fusion(s32[4096]{0:T(1024)S(1)} %bitcast.109, bf16[4096,128]{1,0:T(8,128)(2,1)S(1)} %bitcast.102, bf16[]{:T(256)} %constant.36.clone.1), kind=kCustom, calls=%fused_computation.35 | custom fusion | bytes 8388610 | tf_op jit(solution)/shard_map/scatter | solution.py:41
  444.1 11.6 %copy.58 = bf16[128,4,2,4096]{3,0,2,1:T(8,128)(2,1)} copy(bf16[128,4,2,4096]{0,3,2,1:T(8,128)(2,1)} %bitcast.87) | data formatting | bytes 16777216 | tf_op jit(solution)/shard_map/reshape | solution.py:42
  455.8 71.4 %reduce-scatter.9.cloned.1.call-done = bf16[128,4,2,512]{3,0,2,1:T(8,128)(2,1)} async-done(((bf16[128,4,2,4096]{3,0,2,1:T(8,128)(2,1)}), bf16[128,4,2,512]{3,0,2,1:T(8,128)(2,1)}) %reduce-scatter.9.cloned.1.call-update) | async-done | bytes 1048592 | tf_op jit(solution)/shard_map/reduce_scatter | solution.py:43
  527.2 30.2 %all_to_all.37 = bf16[128,4,2,512]{3,0,2,1:T(8,128)(2,1)S(1)} all-to-all(bf16[128,4,2,512]{3,0,2,1:T(8,128)(2,1)} %reduce-scatter.9.cloned.1.call-done), channel_id=1, replica_groups=mesh['tile'=8,'col'=4] {'col'}, dimensions={1} | all-to-all | bytes 2097152 | tf_op jit(solution)/shard_map/all_to_all | solution.py:46
  558.6 54.1 %all-gather.9.cloned.1.call-done = bf16[512,1,2,4096]{3,0,2,1:T(8,128)(2,1)} async-done(((bf16[512,1,2,512]{3,0,2,1:T(8,128)(2,1)}), bf16[512,1,2,4096]{3,0,2,1:T(8,128)(2,1)}) %all-gather.9.cloned.1.call-update) | async-done | bytes 8388624 | tf_op jit(solution)/shard_map/all_gather | solution.py:47
  612.7 12.2 %copy.60 = bf16[512,1,2,4096]{0,3,2,1:T(8,128)(2,1)} copy(bf16[512,1,2,4096]{3,0,2,1:T(8,128)(2,1)} %all-gather.9.cloned.1.call-done) | data formatting | bytes 16777216 | tf_op jit(solution)/shard_map/all_gather | solution.py:47
  624.9 17.2 %fusion = f32[512,2048]{1,0:T(8,128)} fusion(bf16[2,2048,4096]{2,1,0:T(8,128)(2,1)} %param.5, bf16[512,8192]{0,1:T(8,128)(2,1)} %bitcast.93), kind=kOutput, calls=%fused_computation.5 | convolution fusion | flops 8589934592 | bytes 25165824 | tf_op jit(solution)/shard_map/dot_general | solution.py:54
  642.1 14.1 %fusion.2 = f32[512,2048]{1,0:T(8,128)} fusion(bf16[2,2048,4096]{2,1,0:T(8,128)(2,1)} %param.5, bf16[512,8192]{0,1:T(8,128)(2,1)S(1)} %bitcast.96), kind=kOutput, calls=%fused_computation.7 | convolution fusion | flops 8589934592 | bytes 25165824 | tf_op jit(solution)/shard_map/dot_general | solution.py:54
  656.2 14.6 %add_convert_fusion = bf16[512,2048]{1,0:T(8,128)(2,1)S(1)} fusion(f32[512,2048]{1,0:T(8,128)} %fusion, bf16[2,2048,4096]{2,1,0:T(8,128)(2,1)} %param.5, bf16[512,8192]{0,1:T(8,128)(2,1)} %bitcast.94), kind=kOutput, calls=%fused_computation.31 | convolution fusion | flops 8592031744 | bytes 27262976 | tf_op jit(solution)/shard_map/dot_general | solution.py:54
  670.7 14.3 %subtract_convert_fusion = bf16[512,2048]{1,0:T(8,128)(2,1)S(1)} fusion(f32[512,2048]{1,0:T(8,128)} %fusion.2, bf16[2,2048,4096]{2,1,0:T(8,128)(2,1)} %param.5, bf16[512,8192]{0,1:T(8,128)(2,1)} %bitcast.95), kind=kOutput, calls=%fused_computation.32 | convolution fusion | flops 8592031744 | bytes 27262976 | tf_op jit(solution)/shard_map/dot_general | solution.py:54
  685.1 2.2 pad_maximum_fusion.1
  687.4 76.9 %reduce-scatter.11.cloned.1.call-done = bf16[128,4096]{1,0:T(8,128)(2,1)} async-done(((bf16[512,4096]{1,0:T(8,128)(2,1)}), bf16[128,4096]{1,0:T(8,128)(2,1)}) %reduce-scatter.11.cloned.1.call-update) | async-done | bytes 1048592 | tf_op jit(solution)/shard_map/reduce_scatter | solution.py:58
  764.3 2.1 reshape.165
  766.4 3.1 copy.61
  769.5 54.9 %all-gather.11.cloned.1.call-done = bf16[128,2,16384]{0,1,2:T(2,128)(2,1)} async-done(((bf16[128,2,2048]{0,1,2:T(2,128)(2,1)}), bf16[128,2,16384]{0,1,2:T(2,128)(2,1)}) %all-gather.11.cloned.1.call-update) | async-done | bytes 8388624 | tf_op jit(solution)/shard_map/all_gather | solution.py:65
  824.4 10.4 %gather_fusion.2 = bf16[2048,128,2]{1,2,0:T(2,128)(2,1)S(1)} fusion(bf16[128,2,16384]{0,1,2:T(2,128)(2,1)} %all-gather.11.cloned.1.call-done, s32[2048]{0:T(1024)S(1)} %broadcast_clamp_fusion), kind=kCustom, calls=%fused_computation.2 | custom fusion | bytes 2105344 | tf_op jit(solution)/shard_map/gather | solution.py:67
  (69 shorter events, 19.0 us)
Async XLA Ops:
  7.2 6.1 copy-start.3
  7.2 110.7 %reduce-scatter.5.cloned.1.call-start = ((), (), s32[]{:S(2)}) async-start(), calls=%async_computation.6 | async-start | bytes 9437184 | tf_op jit(solution)/shard_map/reduce_scatter | solution.py:43
  8.6 7.6 copy-start.4
  11.0 5.3 copy-start.7
  43.7 159.6 %all-gather.5.cloned.1.call-start = ((), (), s32[]{:S(2)}) async-start(), calls=%async_computation.7 | async-start | bytes 9437184 | tf_op jit(solution)/shard_map/all_gather | solution.py:47
  149.1 205.7 %reduce-scatter.7.cloned.1.call-start = ((), (), s32[]{:S(2)}) async-start(), calls=%async_computation.8 | async-start | bytes 5242880 | tf_op jit(solution)/shard_map/reduce_scatter | solution.py:58
  215.3 17.2 %copy-start = (bf16[512,1,2,4096]{0,3,2,1:T(8,128)(2,1)S(1)}, bf16[512,1,2,4096]{0,3,2,1:T(8,128)(2,1)}, u32[]{:S(2)}) copy-start(bf16[512,1,2,4096]{0,3,2,1:T(8,128)(2,1)} %copy.52) | copy-start | bytes 25165828
  277.9 136.8 %all-gather.7.cloned.1.call-start = ((), (), s32[]{:S(2)}) async-start(), calls=%async_computation.9 | async-start | bytes 9437184 | tf_op jit(solution)/shard_map/all_gather | solution.py:65
  359.8 167.5 %reduce-scatter.9.cloned.1.call-start = ((), (), s32[]{:S(2)}) async-start(), calls=%async_computation.10 | async-start | bytes 9437184 | tf_op jit(solution)/shard_map/reduce_scatter | solution.py:43
  426.2 1.0 copy-start.5
  426.2 1.2 copy-start.8
  426.2 1.3 copy-start.10
  455.8 156.9 %all-gather.9.cloned.1.call-start = ((), (), s32[]{:S(2)}) async-start(), calls=%async_computation.11 | async-start | bytes 9437184 | tf_op jit(solution)/shard_map/all_gather | solution.py:47
  558.5 205.8 %reduce-scatter.11.cloned.1.call-start = ((), (), s32[]{:S(2)}) async-start(), calls=%async_computation.12 | async-start | bytes 5242880 | tf_op jit(solution)/shard_map/reduce_scatter | solution.py:58
  624.9 17.2 %copy-start.1 = (bf16[512,1,2,4096]{0,3,2,1:T(8,128)(2,1)S(1)}, bf16[512,1,2,4096]{0,3,2,1:T(8,128)(2,1)}, u32[]{:S(2)}) copy-start(bf16[512,1,2,4096]{0,3,2,1:T(8,128)(2,1)} %copy.60) | copy-start | bytes 25165828
  687.3 137.1 %all-gather.11.cloned.1.call-start = ((), (), s32[]{:S(2)}) async-start(), calls=%async_computation.13 | async-start | bytes 9437184 | tf_op jit(solution)/shard_map/all_gather | solution.py:65
  766.4 69.2 %copy-start.2 = (bf16[128,2,2048]{2,1,0:T(2,128)(2,1)}, bf16[128,2,2048]{2,1,0:T(2,128)(2,1)S(1)}, u32[]{:S(2)}) copy-start(bf16[128,2,2048]{2,1,0:T(2,128)(2,1)S(1)} %reshape.165) | copy-start | bytes 3145732
  835.8 1.0 copy-start.6
  835.8 1.2 copy-start.9
  835.8 1.3 copy-start.11
Sparse Core Ops, SparseCore 0:
  43.8 73.9 reduce-scatter.4
  149.2 54.0 all-gather.4
  278.0 76.7 reduce-scatter.6
  359.9 54.7 all-gather.6
  455.9 71.2 reduce-scatter.8
  558.6 53.9 all-gather.8
  687.4 76.7 reduce-scatter.10
  769.6 54.7 all-gather.10
where the time goes:
time: 855 us; the launch traced here: 847 us
  waiting for transfers between devices  517 us (60%)
  matrix products  124 us (15%)
  local copies, waits for them, and re-layouts  121 us (14%)
  blocking collectives  60.3 us (7%)
  between operations  15 us (2%)
  other arithmetic  8.68 us (1%)
    reduce_scatter x2, waiting for transfers between devices, per_device(): lax.psum_scatter(jnp.concatenate([real_part, imag_part], 1).astype(jnp.bf...  154 us
    reduce_scatter x2, waiting for transfers between devices, per_device(): lax.psum_scatter(placed.astype(jnp.float32).astype(jnp.bfloat16), 'tile',...  146 us
    dot_general x8, matrix products, dot_rows(): lax.dot_general(left, right, contract, preferred_element_type=jnp.float32)  121 us
    all_gather x2, waiting for transfers between devices, per_device(): gathered = lax.all_gather(pressure, 'tile', axis=2, tiled=True)  110 us
    all_gather x2, waiting for transfers between devices, per_device(): full_cols = lax.all_gather(moved, 'tile', axis=3, tiled=True)  108 us
    all_to_all x2, blocking collectives, per_device(): lax.all_to_all(shares, 'col', split_axis=1, concat_axis=0, tiled=True)  60.3 us
    scatter x2, local copies, waits for them, and re-layouts, per_device(): jnp.zeros((loads_dev, 2 * patch_count), jnp.bfloat16).at[:, flat_index]  31.5 us
    all_gather x2, local copies, waits for them, and re-layouts, per_device(): full_cols = lax.all_gather(moved, 'tile', axis=3, tiled=True)  24.2 us
  transfers between devices with their start and end apart: 8, of which 8 were waited for; matrix products, arithmetic and copies ran while one was open for 0% of the time, Pallas kernels for 0%

commit v1 on v0

v1 whole, which is shorter than its diff:
```python
import functools

import jax
import jax.numpy as jnp
from jax import lax
from jax.experimental import pallas as pl
from jax.experimental.pallas import tpu as pltpu
from jax.sharding import PartitionSpec as P

ITERS = 2
LANES = 128
BF16 = jnp.bfloat16
F32 = jnp.float32


def pick_kernel(index_ref, rows_ref, out_ref):
    count = out_ref.shape[0]
    step = 16

    @pl.loop(0, count // step)
    def _(block):
        base = block * step
        for k in range(step):
            out_ref[base + k] = rows_ref[index_ref[base + k]]


def pick_rows(index, rows):
    return pl.pallas_call(
        pick_kernel,
        out_shape=jax.ShapeDtypeStruct((index.shape[0],) + rows.shape[1:], rows.dtype),
        in_specs=[
            pl.BlockSpec(memory_space=pltpu.SMEM),
            pl.BlockSpec(memory_space=pltpu.VMEM),
        ],
        out_specs=pl.BlockSpec(memory_space=pltpu.VMEM),
        compiler_params=pltpu.CompilerParams(vmem_limit_bytes=40 * 2**20),
    )(index, rows)


def product_kernel(z_ref, x_ref, out_ref):
    groups, _, width = out_ref.shape
    half = width // 2
    a = jnp.dot(z_ref[0], x_ref[...], preferred_element_type=F32)
    b = jnp.dot(z_ref[1], x_ref[...], preferred_element_type=F32)
    for g in range(groups):
        re = slice(g * width, g * width + half)
        im = slice(g * width + half, (g + 1) * width)
        out_ref[g] = jnp.concatenate([a[:, re] - b[:, im], a[:, im] + b[:, re]], 1).astype(out_ref.dtype)


def product(impedance, x, groups):
    _, rows, depth = impedance.shape
    width = x.shape[1] // groups
    block = min(256, rows)
    return pl.pallas_call(
        product_kernel,
        grid=(rows // block,),
        out_shape=jax.ShapeDtypeStruct((groups, rows, width), BF16),
        in_specs=[
            pl.BlockSpec((2, block, depth), lambda i: (0, i, 0)),
            pl.BlockSpec((depth, groups * width), lambda i: (0, 0)),
        ],
        out_specs=pl.BlockSpec((groups, block, width), lambda i: (0, i, 0)),
        compiler_params=pltpu.CompilerParams(vmem_limit_bytes=48 * 2**20),
    )(impedance, x)


def inverse_permutation(sigma):
    count = sigma.shape[0]
    where = jnp.arange(count, dtype=jnp.int32)
    high = (sigma // LANES)[None, :] == jnp.arange(count // LANES, dtype=jnp.int32)[:, None]
    low = (sigma % LANES)[:, None] == jnp.arange(LANES, dtype=jnp.int32)[None, :]
    where_high = jnp.where(low, (where // LANES)[:, None], 0).astype(BF16)
    where_low = jnp.where(low, (where % LANES)[:, None], 0).astype(BF16)
    digits = jnp.dot(
        high.astype(BF16), jnp.concatenate([where_high, where_low], 1), preferred_element_type=F32
    )
    inverse = digits[:, :LANES] * LANES + digits[:, LANES:]
    return inverse.astype(jnp.int32).reshape(count)


def per_device(impedance, mobility, force, patch_map, ownership):
    slots, width, _ = mobility.shape
    patches = patch_map.shape[0]
    loads = force.shape[0]
    tiles = lax.axis_size("tile")
    cols = lax.axis_size("col")
    share = patches // cols // tiles
    mine = slots * width
    tile = lax.axis_index("tile")

    panels = patch_map.reshape(-1, width)
    slot_flat = panels[ownership].reshape(mine)
    owners = lax.all_gather(ownership, "tile", axis=0, tiled=True)
    inverse = inverse_permutation(panels[owners].reshape(patches))
    share_index = lax.dynamic_index_in_dim(
        inverse.reshape(cols, tiles, share), tile, 1, keepdims=False
    ).reshape(cols * share)

    mob_re = mobility[:, :, :width]
    mob_im = mobility[:, :, width:]
    form = jnp.stack(
        [jnp.stack([mob_re, -mob_im], -1), jnp.stack([mob_im, mob_re], -1)], 2
    ).reshape(slots, 2 * width, 2 * width)
    force_rows = force.reshape(loads, slots, 2, width).transpose(1, 3, 2, 0).reshape(slots, 2 * width, loads)

    def response(drive):
        return lax.dot_general(
            form, drive, (((2,), (1,)), ((0,), (0,))), preferred_element_type=F32
        ).astype(BF16)

    velocity = response(force_rows)
    for _ in range(ITERS):
        everyone = lax.all_gather(velocity.reshape(mine, 2, loads), "tile", axis=0, tiled=True)
        picked = pick_rows(share_index, everyone).reshape(cols, share, 2, loads)
        moved = lax.all_to_all(picked, "col", split_axis=0, concat_axis=0, tiled=True)
        columns = moved.transpose(1, 0, 2, 3).reshape(share, cols * 2 * loads)
        field = lax.all_gather(columns, "tile", axis=0, tiled=True)
        partial = product(impedance, field, cols)
        summed = lax.psum_scatter(partial, "col", scatter_dimension=0, tiled=True)
        pressure = summed.reshape(-1, 2, loads)
        gathered = lax.all_gather(pressure, "tile", axis=0, tiled=True)
        at_slots = pick_rows(slot_flat, gathered).reshape(slots, 2 * width, loads)
        drive = (force_rows.astype(F32) - at_slots.astype(F32)).astype(BF16)
        velocity = response(drive)
    velocity_out = velocity.reshape(slots, width, 2, loads).transpose(3, 0, 2, 1).reshape(loads, slots, 2 * width)
    pressure_out = pressure.transpose(2, 1, 0)
    return velocity_out, pressure_out


def solution(mesh):
    return jax.shard_map(
        per_device,
        mesh=mesh,
        in_specs=(
            P(None, "tile", "col"),
            P("tile", None, None),
            P("col", "tile", None),
            P(),
            P("tile"),
        ),
        out_specs=(P("col", "tile", None), P("col", None, "tile")),
        check_vma=False,
    )
```

time: 855 us -> 701 us (0.82)
  matrix products: 124 us -> 5.47 us
  Pallas kernels: 0 us -> 93.2 us
  local copies, waits for them, and re-layouts: 121 us -> 49 us
  waiting for transfers between devices: 517 us -> 454 us
  blocking collectives: 60.3 us -> 70.6 us
    reduce_scatter x4 -> x2, waiting for transfers between devices: 299 us -> 154 us  [per_device(): summed = lax.psum_scatter(partial, 'col', scatter_dimension=0, tiled=True)]
    dot_general x11 -> x4, matrix products: 124 us -> 5.47 us  [the longest x3 4.22 us: response(): lax.dot_general(form, drive, (((2,), (1,)), ((0,), (0,))), preferred_elem...]
    pallas_call x0 -> x6, Pallas kernels: none -> 93.2 us  [the longest x2 81.9 us: product(): pl.pallas_call(product_kernel, grid=(rows // block,), out_shape=jax.Shape...]
    all_gather x4 -> x6, waiting for transfers between devices: 218 us -> 300 us  [the longest x2 105 us: per_device(): field = lax.all_gather(columns, 'tile', axis=0, tiled=True)]
    scatter x2 -> x0, local copies, waits for them, and re-layouts: 31.5 us -> none  [per_device(): jnp.zeros((loads_dev, 2 * patch_count), jnp.bfloat16).at[:, flat_index]]
    all_gather x2 -> x0, local copies, waits for them, and re-layouts: 24.2 us -> none  [per_device(): full_cols = lax.all_gather(moved, 'tile', axis=3, tiled=True)]
    reshape x9, local copies, waits for them, and re-layouts: 34.4 us -> 11.9 us  [the longest x2 4.26 us: per_device(): pressure = summed.reshape(-1, 2, loads)]
    unnamed x26, local copies, waits for them, and re-layouts: 4.19 us -> 25.7 us
  transfers between devices with their start and end apart: 8 -> 8, of which waited for: 8 -> 8; matrix products, arithmetic and copies ran while one was open for 0% -> 2% of each run, Pallas kernels for 0% -> 0%
where the time goes in v1:
time: 701 us
  waiting for transfers between devices  454 us (65%)
  Pallas kernels  93.2 us (13%)
  blocking collectives  70.6 us (10%)
  local copies, waits for them, and re-layouts  49 us (7%)
  between operations  15.1 us (2%)
  other arithmetic  13.5 us (2%)
    reduce_scatter x2, waiting for transfers between devices, per_device(): summed = lax.psum_scatter(partial, 'col', scatter_dimension=0, tiled=True)  154 us
    all_gather x2, waiting for transfers between devices, per_device(): field = lax.all_gather(columns, 'tile', axis=0, tiled=True)  105 us
    all_gather x2, waiting for transfers between devices, per_device(): gathered = lax.all_gather(pressure, 'tile', axis=0, tiled=True)  104 us
    all_gather x2, waiting for transfers between devices, per_device(): lax.all_gather(velocity.reshape(mine, 2, loads), 'tile', axis=0, tiled=True)  90.3 us
    pallas_call x2, Pallas kernels, product(): pl.pallas_call(product_kernel, grid=(rows // block,), out_shape=jax.Shape...  81.9 us
    all_to_all x2, blocking collectives, per_device(): lax.all_to_all(picked, 'col', split_axis=0, concat_axis=0, tiled=True)  61.1 us
    unnamed x26, local copies, waits for them, and re-layouts  25.7 us
  transfers between devices with their start and end apart: 8, of which 8 were waited for; matrix products, arithmetic and copies ran while one was open for 2% of the time, Pallas kernels for 0%

profile of v1, /device:TPU:0, one launch (start us, length us, event | category | flops | bytes accessed | tf_op | source)
XLA Modules:
  0.0 700.8 jit_solution(17494632408659288802)
XLA Ops:
  9.6 7.9 %copy.39 = bf16[32,64,2,64,2]{0,4,3,2,1:T(2,128)(2,1)} copy(bf16[32,64,2,64,2]{3,1,0,4,2:T(8,128)(2,1)S(1)} %pad_maximum_fusion) | data formatting | bytes 2097152 | tf_op jit(solution)/shard_map/stack | solution.py:102
  17.5 4.1 copy.50
  23.3 1.7 convolution_convert_fusion.2
  26.7 9.5 %all-reduce = s32[256]{0:T(256)S(1)} all-reduce(s32[256]{0:T(256)S(1)} %dynamic-update-slice), channel_id=1, replica_groups=mesh['tile'=8,'col'=4] {'tile'}, use_global_device_ids=true, to_apply=%add | all-reduce | flops 256 | bytes 2048
  37.2 7.8 %select_convert_fusion.1 = (bf16[16384,128]{1,0:T(8,128)(2,1)S(1)}, bf16[16384,128]{1,0:T(8,128)(2,1)S(1)}) fusion(s32[16384]{0:T(1024)S(1)} %get-tuple-element.20, s32[16384]{0:T(1024)S(1)} %get-tuple-element.16, s32[16384]{0:T(1024)S(1)} %get-tuple-element.19), kind=kLoop, calls=%fused_computation.7 | loop fusion | flops 10485760 | bytes 8585216 | tf_op jit(solution)/shard_map/convert_element_type | solution.py:73
  46.3 35.9 %all-gather.7.cloned.1.call-done.rows_ref = bf16[16384,2,128]{2,1,0:T(2,128)(2,1)} async-done(((bf16[2048,2,128]{2,1,0:T(2,128)(2,1)}), bf16[16384,2,128]{2,1,0:T(2,128)(2,1)}) %all-gather.7.cloned.1.call-update) | async-done | bytes 8388624 | tf_op jit(solution)/shard_map/all_gather | solution.py:114
  82.2 3.4 copy-done.2
  85.6 2.8 shard_map.68
  88.4 30.5 %all_to_all.10 = bf16[4,512,2,128]{3,2,1,0:T(2,128)(2,1)S(1)} all-to-all(bf16[4,512,2,128]{3,2,1,0:T(2,128)(2,1)S(1)} %bitcast.44), channel_id=1, replica_groups=mesh['tile'=8,'col'=4] {'col'}, dimensions={0} | all-to-all | bytes 2097152 | tf_op jit(solution)/shard_map/all_to_all | solution.py:116
  121.3 52.5 %all-gather.9.cloned.1.call-done.x_ref = bf16[4096,1024]{1,0:T(8,128)(2,1)} async-done(((bf16[512,1024]{1,0:T(8,128)(2,1)}), bf16[4096,1024]{1,0:T(8,128)(2,1)}) %all-gather.9.cloned.1.call-update) | async-done | bytes 8388624 | tf_op jit(solution)/shard_map/all_gather | solution.py:118
  173.8 40.9 %shard_map.69 = bf16[4,2048,256]{2,1,0:T(8,128)(2,1)S(1)} custom-call(bf16[2,2048,4096]{2,1,0:T(8,128)(2,1)} %z_ref.3, bf16[4096,1024]{1,0:T(8,128)(2,1)} %all-gather.9.cloned.1.call-done.x_ref), custom_call_target="tpu_custom_call" | custom-call | tf_op jit(solution)/shard_map/pallas_call | solution.py:55
  214.8 1.9 copy-done
  216.8 76.9 %reduce-scatter.3.cloned.1.call-done = bf16[1,2048,256]{2,1,0:T(8,128)(2,1)} async-done(((bf16[4,2048,256]{2,1,0:T(8,128)(2,1)}), bf16[1,2048,256]{2,1,0:T(8,128)(2,1)}) %reduce-scatter.3.cloned.1.call-update) | async-done | bytes 1048592 | tf_op jit(solution)/shard_map/reduce_scatter | solution.py:120
  293.7 2.1 reshape.143
  296.7 54.0 %all-gather.11.cloned.1.call-done.rows_ref = bf16[16384,2,128]{2,1,0:T(2,128)(2,1)} async-done(((bf16[2048,2,128]{2,1,0:T(2,128)(2,1)}), bf16[16384,2,128]{2,1,0:T(2,128)(2,1)}) %all-gather.11.cloned.1.call-update) | async-done | bytes 8388624 | tf_op jit(solution)/shard_map/all_gather | solution.py:122
  350.8 3.4 copy-done.3
  354.2 2.8 shard_map.70
  358.6 1.7 convolution_convert_fusion.1
  360.4 54.4 %all-gather.13.cloned.1.call-done.rows_ref = bf16[16384,2,128]{2,1,0:T(2,128)(2,1)} async-done(((bf16[2048,2,128]{2,1,0:T(2,128)(2,1)}), bf16[16384,2,128]{2,1,0:T(2,128)(2,1)}) %all-gather.13.cloned.1.call-update) | async-done | bytes 8388624 | tf_op jit(solution)/shard_map/all_gather | solution.py:114
  414.8 3.4 copy-done.4
  418.1 2.8 shard_map.71
  421.0 30.5 %all_to_all.11 = bf16[4,512,2,128]{3,2,1,0:T(2,128)(2,1)S(1)} all-to-all(bf16[4,512,2,128]{3,2,1,0:T(2,128)(2,1)S(1)} %bitcast.43), channel_id=1, replica_groups=mesh['tile'=8,'col'=4] {'col'}, dimensions={0} | all-to-all | bytes 2097152 | tf_op jit(solution)/shard_map/all_to_all | solution.py:116
  453.9 52.5 %all-gather.15.cloned.1.call-done.x_ref = bf16[4096,1024]{1,0:T(8,128)(2,1)} async-done(((bf16[512,1024]{1,0:T(8,128)(2,1)}), bf16[4096,1024]{1,0:T(8,128)(2,1)}) %all-gather.15.cloned.1.call-update) | async-done | bytes 8388624 | tf_op jit(solution)/shard_map/all_gather | solution.py:118
  506.3 40.9 %shard_map.72 = bf16[4,2048,256]{2,1,0:T(8,128)(2,1)S(1)} custom-call(bf16[2,2048,4096]{2,1,0:T(8,128)(2,1)} %z_ref.3, bf16[4096,1024]{1,0:T(8,128)(2,1)} %all-gather.15.cloned.1.call-done.x_ref), custom_call_target="tpu_custom_call" | custom-call | tf_op jit(solution)/shard_map/pallas_call | solution.py:55
  547.3 1.9 copy-done.1
  549.3 76.9 %reduce-scatter.5.cloned.1.call-done = bf16[1,2048,256]{2,1,0:T(8,128)(2,1)} async-done(((bf16[4,2048,256]{2,1,0:T(8,128)(2,1)}), bf16[1,2048,256]{2,1,0:T(8,128)(2,1)}) %reduce-scatter.5.cloned.1.call-update) | async-done | bytes 1048592 | tf_op jit(solution)/shard_map/reduce_scatter | solution.py:120
  626.2 2.1 reshape.147
  628.4 4.8 copy.54
  633.1 50.3 %all-gather.17.cloned.1.call-done.rows_ref = bf16[16384,2,128]{2,1,0:T(2,128)(2,1)} async-done(((bf16[2048,2,128]{2,1,0:T(2,128)(2,1)}), bf16[16384,2,128]{2,1,0:T(2,128)(2,1)}) %all-gather.17.cloned.1.call-update) | async-done | bytes 8388624 | tf_op jit(solution)/shard_map/all_gather | solution.py:122
  683.5 3.4 copy-done.5
  686.8 2.8 shard_map.73
  692.3 1.7 copy.53
  (63 shorter events, 17.2 us)
Async XLA Ops:
  7.2 75.0 %all-gather.7.cloned.1.call-start = ((), (), s32[]{:S(2)}) async-start(), calls=%async_computation.4 | async-start | bytes 9437184 | tf_op jit(solution)/shard_map/all_gather | solution.py:114
  17.5 4.1 copy-start.6
  21.6 3.5 copy-start.7
  21.6 3.6 copy-start.9
  21.6 4.9 copy-start.8
  25.1 148.7 %all-gather.9.cloned.1.call-start = ((), (), s32[]{:S(2)}) async-start(), calls=%async_computation.5 | async-start | bytes 9437184 | tf_op jit(solution)/shard_map/all_gather | solution.py:118
  82.2 3.4 copy-start.2
  121.3 172.4 %reduce-scatter.3.cloned.1.call-start = ((), (), s32[]{:S(2)}) async-start(), calls=%async_computation.6 | async-start | bytes 5242880 | tf_op jit(solution)/shard_map/reduce_scatter | solution.py:120
  214.7 2.0 copy-start
  216.7 134.1 %all-gather.11.cloned.1.call-start = ((), (), s32[]{:S(2)}) async-start(), calls=%async_computation.7 | async-start | bytes 9437184 | tf_op jit(solution)/shard_map/all_gather | solution.py:122
  295.8 118.9 %all-gather.13.cloned.1.call-start = ((), (), s32[]{:S(2)}) async-start(), calls=%async_computation.8 | async-start | bytes 9437184 | tf_op jit(solution)/shard_map/all_gather | solution.py:114
  350.8 3.4 copy-start.3
  360.3 146.0 %all-gather.15.cloned.1.call-start = ((), (), s32[]{:S(2)}) async-start(), calls=%async_computation.9 | async-start | bytes 9437184 | tf_op jit(solution)/shard_map/all_gather | solution.py:118
  414.8 3.4 copy-start.4
  453.8 172.4 %reduce-scatter.5.cloned.1.call-start = ((), (), s32[]{:S(2)}) async-start(), calls=%async_computation.10 | async-start | bytes 5242880 | tf_op jit(solution)/shard_map/reduce_scatter | solution.py:120
  547.3 2.0 copy-start.1
  549.3 134.2 %all-gather.17.cloned.1.call-start = ((), (), s32[]{:S(2)}) async-start(), calls=%async_computation.11 | async-start | bytes 9437184 | tf_op jit(solution)/shard_map/all_gather | solution.py:122
  683.5 3.4 copy-start.5
Sparse Core Ops, SparseCore 0:
  25.2 56.9 all-gather.6
  121.4 52.3 all-gather.8
  216.8 76.7 reduce-scatter.2
  296.0 54.7 all-gather.10
  360.5 54.2 all-gather.12
  453.9 52.3 all-gather.14
  549.4 76.7 reduce-scatter.4
  628.7 54.7 all-gather.16

commit v2 on v1

--- a/solution.py
+++ b/solution.py
@@ -13,55 +13,235 @@
 F32 = jnp.float32
 
 
-def pick_kernel(index_ref, rows_ref, out_ref):
+MESH = pl.DeviceIdType.MESH
+
+
+def gather_over_tile(tiles, x_ref, buf, send_sem, recv_sem, own_sem, ready):
+    a_size = tiles // 4
+    rows = x_ref.shape[0]
+    half = rows // 2
+    me = lax.axis_index("tile")
+    core = lax.rem(me, 2)
+    my_b = lax.rem(me // 2, 2)
+    my_a = me // 4
+    others = range(1, a_size)
+
+    def chip_at(oa, ob):
+        return lax.rem(my_a + oa, a_size) * 2 + lax.rem(my_b + ob, 2)
+
+    def device_at(oa, ob):
+        return chip_at(oa, ob) * 2 + core
+
+    partner = chip_at(0, 0) * 2 + 1 - core
+    neighbours = [partner, device_at(0, 1)] + [device_at(o, 0) for o in others]
+
+    barrier = pltpu.get_barrier_semaphore()
+    for device in neighbours:
+        pl.semaphore_signal(barrier, inc=1, device_id={"tile": device}, device_id_type=MESH)
+    pl.semaphore_wait(barrier, len(neighbours))
+
+    def piece(oa, ob, h, owner_core):
+        return buf.at[chip_at(oa, ob), pl.ds(pl.multiple_of(owner_core * rows + h * half, half), half)]
+
+    sent = []
+
+    def send(src, dst, device, relayed, oa, ob, h):
+        copy = pltpu.make_async_remote_copy(
+            src_ref=src,
+            dst_ref=dst,
+            send_sem=send_sem.at[len(sent)],
+            recv_sem=recv_sem.at[relayed, oa * 2 + ob, h],
+            device_id={"tile": device},
+            device_id_type=MESH,
+        )
+        copy.start()
+        sent.append(copy)
+
+    def arrived(relayed, oa, ob, h):
+        slot = piece(oa, ob, h, 1 - core if relayed else core)
+        pltpu.make_async_remote_copy(
+            src_ref=slot,
+            dst_ref=slot,
+            send_sem=send_sem.at[0],
+            recv_sem=recv_sem.at[relayed, oa * 2 + ob, h],
+            device_id={"tile": partner},
+            device_id_type=MESH,
+        ).wait_recv()
+
+    def relay(oa, ob, h):
+        slot = piece(oa, ob, h, core)
+        send(slot, slot, partner, 1, oa, ob, h)
+
+    def forward(oa, ob, h, device, new_oa, new_ob):
+        slot = piece(oa, ob, h, core)
+        send(slot, slot, device, 0, new_oa, new_ob, h)
+
+    def own(h):
+        return x_ref.at[pl.ds(h * half, half)]
+
+    for h in (1, 0):
+        send(own(h), piece(0, 0, h, core), device_at(0, 1), 0, 0, 1, h)
+    for h in (0, 1):
+        for o in others:
+            send(own(h), piece(0, 0, h, core), device_at(o, 0), 0, (a_size - o) % a_size, 0, h)
+    for h in (0, 1):
+        send(own(h), piece(0, 0, h, core), partner, 1, 0, 0, h)
+    local = pltpu.make_async_copy(
+        x_ref, buf.at[chip_at(0, 0), pl.ds(pl.multiple_of(core * rows, rows), rows)], own_sem.at[0]
+    )
+    local.start()
+    local.wait()
+    for h in (0, 1):
+        arrived(1, 0, 0, h)
+    ready(chip_at(0, 0))
+
+    arrived(0, 0, 1, 1)
+    for o in others:
+        forward(0, 1, 1, device_at(o, 0), (a_size - o) % a_size, 1)
+    for o in others:
+        arrived(0, o, 0, 0)
+        forward(o, 0, 0, device_at(0, 1), o, 1)
+    relay(0, 1, 1)
+    for o in others:
+        relay(o, 0, 0)
+    arrived(0, 0, 1, 0)
+    relay(0, 1, 0)
+    for o in others:
+        arrived(0, o, 0, 1)
+        relay(o, 0, 1)
+    for h in (1, 0):
+        arrived(1, 0, 1, h)
+    ready(chip_at(0, 1))
+    for o in others:
+        for h in (0, 1):
+            arrived(0, o, 1, h)
+            relay(o, 1, h)
+    for o in others:
+        for h in (0, 1):
+            arrived(1, o, 0, h)
+        ready(chip_at(o, 0))
+    for o in others:
+        for h in (0, 1):
+            arrived(1, o, 1, h)
+        ready(chip_at(o, 1))
+    for copy in sent:
+        copy.wait_send()
+
+
+def chip_order(tiles):
+    a_size = tiles // 4
+    me = lax.axis_index("tile")
+    my_b = lax.rem(me // 2, 2)
+    my_a = me // 4
+    order = [(0, 0), (0, 1)] + [(o, b) for b in (0, 1) for o in range(1, a_size)]
+    return [lax.rem(my_a + oa, a_size) * 2 + lax.rem(my_b + ob, 2) for oa, ob in order]
+
+
+def gather_scratch(tiles, shape):
+    a_size = tiles // 4
+    copies = 2 + 2 * (a_size - 1) + 2 * (a_size - 1) + 2 * 2 * a_size
+    return [
+        pltpu.VMEM((tiles // 2, 2 * shape[0]) + shape[1:], BF16),
+        pltpu.SemaphoreType.DMA((copies,)),
+        pltpu.SemaphoreType.DMA((2, 2 * a_size, 2)),
+        pltpu.SemaphoreType.DMA((1,)),
+    ]
+
+
+def pick_kernel(tiles, index_ref, x_ref, out_ref, buf, send_sem, recv_sem, own_sem):
+    gather_over_tile(tiles, x_ref, buf, send_sem, recv_sem, own_sem, lambda chip: None)
     count = out_ref.shape[0]
+    pair = buf.shape[1]
     step = 16
 
     @pl.loop(0, count // step)
     def _(block):
         base = block * step
         for k in range(step):
-            out_ref[base + k] = rows_ref[index_ref[base + k]]
-
-
-def pick_rows(index, rows):
+            index = index_ref[base + k]
+            out_ref[base + k] = buf[index // pair, lax.rem(index, pair)]
+
+
+def gather_and_pick(index, rows, tiles):
     return pl.pallas_call(
-        pick_kernel,
+        functools.partial(pick_kernel, tiles),
         out_shape=jax.ShapeDtypeStruct((index.shape[0],) + rows.shape[1:], rows.dtype),
         in_specs=[
             pl.BlockSpec(memory_space=pltpu.SMEM),
             pl.BlockSpec(memory_space=pltpu.VMEM),
         ],
         out_specs=pl.BlockSpec(memory_space=pltpu.VMEM),
-        compiler_params=pltpu.CompilerParams(vmem_limit_bytes=40 * 2**20),
+        scratch_shapes=gather_scratch(tiles, rows.shape),
+        compiler_params=pltpu.CompilerParams(
+            collective_id=0, has_side_effects=True, vmem_limit_bytes=40 * 2**20
+        ),
     )(index, rows)
 
 
-def product_kernel(z_ref, x_ref, out_ref):
-    groups, _, width = out_ref.shape
+def product_kernel(tiles, z_ref, x_ref, out_ref, z_buf, z_sem, total, buf, send_sem, recv_sem, own_sem):
+    groups, rows, width = out_ref.shape
     half = width // 2
-    a = jnp.dot(z_ref[0], x_ref[...], preferred_element_type=F32)
-    b = jnp.dot(z_ref[1], x_ref[...], preferred_element_type=F32)
-    for g in range(groups):
-        re = slice(g * width, g * width + half)
-        im = slice(g * width + half, (g + 1) * width)
-        out_ref[g] = jnp.concatenate([a[:, re] - b[:, im], a[:, im] + b[:, re]], 1).astype(out_ref.dtype)
-
-
-def product(impedance, x, groups):
+    depth = z_buf.shape[3]
+    block = min(256, rows)
+    chips = chip_order(tiles)
+    steps = len(chips)
+
+    def fetch(step):
+        start = pl.multiple_of(chips[step] * depth, depth)
+        return pltpu.make_async_copy(z_ref.at[:, :, pl.ds(start, depth)], z_buf.at[step % 2], z_sem.at[step % 2])
+
+    for step in range(min(2, steps)):
+        fetch(step).start()
+    done = []
+
+    def ready(chip):
+        step = len(done)
+        done.append(step)
+        fetch(step).wait()
+
+        @pl.loop(0, rows // block)
+        def _(i):
+            at = pl.ds(pl.multiple_of(i * block, block), block)
+            x = buf[chip]
+            a = jnp.dot(z_buf[step % 2, 0, at, :], x, preferred_element_type=F32)
+            b = jnp.dot(z_buf[step % 2, 1, at, :], x, preferred_element_type=F32)
+            for g in range(groups):
+                re = slice(g * width, g * width + half)
+                im = slice(g * width + half, (g + 1) * width)
+                term = jnp.concatenate([a[:, re] - b[:, im], a[:, im] + b[:, re]], 1)
+                if step > 0:
+                    term = total[g, at, :] + term
+                if step < steps - 1:
+                    total[g, at, :] = term
+                else:
+                    out_ref[g, at, :] = term.astype(out_ref.dtype)
+
+        if step + 2 < steps:
+            fetch(step + 2).start()
+
+    gather_over_tile(tiles, x_ref, buf, send_sem, recv_sem, own_sem, ready)
+
+
+def gather_and_multiply(impedance, x, groups, tiles):
     _, rows, depth = impedance.shape
     width = x.shape[1] // groups
-    block = min(256, rows)
     return pl.pallas_call(
-        product_kernel,
-        grid=(rows // block,),
+        functools.partial(product_kernel, tiles),
         out_shape=jax.ShapeDtypeStruct((groups, rows, width), BF16),
         in_specs=[
-            pl.BlockSpec((2, block, depth), lambda i: (0, i, 0)),
-            pl.BlockSpec((depth, groups * width), lambda i: (0, 0)),
+            pl.BlockSpec(memory_space=pl.ANY),
+            pl.BlockSpec(memory_space=pltpu.VMEM),
         ],
-        out_specs=pl.BlockSpec((groups, block, width), lambda i: (0, i, 0)),
-        compiler_params=pltpu.CompilerParams(vmem_limit_bytes=48 * 2**20),
+        out_specs=pl.BlockSpec(memory_space=pltpu.VMEM),
+        scratch_shapes=[
+            pltpu.VMEM((2, 2, rows, 2 * x.shape[0]), BF16),
+            pltpu.SemaphoreType.DMA((2,)),
+            pltpu.VMEM((groups, rows, width), F32),
+        ]
+        + gather_scratch(tiles, x.shape),
+        compiler_params=pltpu.CompilerParams(
+            collective_id=1, has_side_effects=True, vmem_limit_bytes=60 * 2**20
+        ),
     )(impedance, x)
 
 
@@ -111,16 +291,14 @@
 
     velocity = response(force_rows)
     for _ in range(ITERS):
-        everyone = lax.all_gather(velocity.reshape(mine, 2, loads), "tile", axis=0, tiled=True)
-        picked = pick_rows(share_index, everyone).reshape(cols, share, 2, loads)
+        picked = gather_and_pick(share_index, velocity.reshape(mine, 2, loads), tiles)
+        picked = picked.reshape(cols, share, 2, loads)
         moved = lax.all_to_all(picked, "col", split_axis=0, concat_axis=0, tiled=True)
         columns = moved.transpose(1, 0, 2, 3).reshape(share, cols * 2 * loads)
-        field = lax.all_gather(columns, "tile", axis=0, tiled=True)
-        partial = product(impedance, field, cols)
+        partial = gather_and_multiply(impedance, columns, cols, tiles)
         summed = lax.psum_scatter(partial, "col", scatter_dimension=0, tiled=True)
         pressure = summed.reshape(-1, 2, loads)
-        gathered = lax.all_gather(pressure, "tile", axis=0, tiled=True)
-        at_slots = pick_rows(slot_flat, gathered).reshape(slots, 2 * width, loads)
+        at_slots = gather_and_pick(slot_flat, pressure, tiles).reshape(slots, 2 * width, loads)
         drive = (force_rows.astype(F32) - at_slots.astype(F32)).astype(BF16)
         velocity = response(drive)
     velocity_out = velocity.reshape(slots, width, 2, loads).transpose(3, 0, 2, 1).reshape(loads, slots, 2 * width)

time: 701 us -> 612 us (0.87)
  waiting for transfers between devices: 454 us -> 152 us
  Pallas kernels: 93.2 us -> 327 us
  local copies, waits for them, and re-layouts: 49 us -> 31.2 us
    all_gather x6 -> x0, waiting for transfers between devices: 300 us -> none  [the longest x2 105 us: per_device(): field = lax.all_gather(columns, 'tile', axis=0, tiled=True)]
    pallas_call x6, Pallas kernels: 93.2 us -> 327 us  [the longest x4 207 us: gather_and_pick(): pl.pallas_call(functools.partial(pick_kernel, tiles), out_shape=jax.Shape...]
    unnamed x26 -> x12, local copies, waits for them, and re-layouts: 25.7 us -> 8.9 us
  transfers between devices with their start and end apart: 8 -> 2, of which waited for: 8 -> 2; matrix products, arithmetic and copies ran while one was open for 2% -> 0% of each run, Pallas kernels for 0% -> 0%
where the time goes in v2:
time: 612 us
  Pallas kernels  327 us (53%)
  waiting for transfers between devices  152 us (25%)
  blocking collectives  71.1 us (12%)
  local copies, waits for them, and re-layouts  31.2 us (5%)
  between operations  15 us (2%)
  other arithmetic  12.3 us (2%)
    pallas_call x4, Pallas kernels, gather_and_pick(): pl.pallas_call(functools.partial(pick_kernel, tiles), out_shape=jax.Shape...  207 us
    reduce_scatter x2, waiting for transfers between devices, per_device(): summed = lax.psum_scatter(partial, 'col', scatter_dimension=0, tiled=True)  152 us
    pallas_call x2, Pallas kernels, gather_and_multiply(): pl.pallas_call(functools.partial(product_kernel, tiles), out_shape=jax.Sh...  120 us
    all_to_all x2, blocking collectives, per_device(): lax.all_to_all(picked, 'col', split_axis=0, concat_axis=0, tiled=True)  61.6 us
  transfers between devices with their start and end apart: 2, of which 2 were waited for; matrix products, arithmetic and copies ran while one was open for 0% of the time, Pallas kernels for 0%

profile of v2, /device:TPU:0, one launch (start us, length us, event | category | flops | bytes accessed | tf_op | source)
XLA Modules:
  0.0 611.9 jit_solution(12387033931931515888)
XLA Ops:
  7.2 0.9 reshape.136
  8.2 1.2 dynamic-slice
  10.1 0.9 dynamic-update-slice
  10.9 9.5 %all-reduce = s32[256]{0:T(256)S(1)} all-reduce(s32[256]{0:T(256)S(1)} %dynamic-update-slice), channel_id=1, replica_groups=mesh['tile'=8,'col'=4] {'tile'}, use_global_device_ids=true, to_apply=%add | all-reduce | flops 256 | bytes 2048
  20.4 0.7 gather_fusion.1
  21.3 7.8 %select_convert_fusion.1 = (bf16[16384,128]{1,0:T(8,128)(2,1)S(1)}, bf16[16384,128]{1,0:T(8,128)(2,1)S(1)}) fusion(s32[16384]{0:T(1024)S(1)} %get-tuple-element.20, s32[16384]{0:T(1024)S(1)} %get-tuple-element.16, s32[16384]{0:T(1024)S(1)} %get-tuple-element.19), kind=kLoop, calls=%fused_computation.7 | loop fusion | flops 10485760 | bytes 8585216 | tf_op jit(solution)/shard_map/convert_element_type | solution.py:253
  29.1 1.2 fusion
  31.6 7.7 %copy.39 = bf16[32,64,2,64,2]{0,4,3,2,1:T(2,128)(2,1)} copy(bf16[32,64,2,64,2]{3,1,0,4,2:T(8,128)(2,1)S(1)} %pad_maximum_fusion) | data formatting | bytes 2097152 | tf_op jit(solution)/shard_map/stack | solution.py:282
  39.4 4.1 copy.50
  43.5 1.0 copy.40
  45.2 0.8 convolution_convert_fusion.2
  45.9 51.2 %shard_map.68 = bf16[2048,2,128]{2,1,0:T(2,128)(2,1)S(1)} custom-call(s32[2048]{0:T(1024)S(1)} %bitcast.48, bf16[2048,2,128]{2,1,0:T(2,128)(2,1)S(1)} %bitcast.45), custom_call_target="tpu_custom_call" | custom-call | tf_op jit(solution)/shard_map/pallas_call | solution.py:166
  97.1 31.0 %all_to_all.10 = bf16[4,512,2,128]{3,2,1,0:T(2,128)(2,1)S(1)} all-to-all(bf16[4,512,2,128]{3,2,1,0:T(2,128)(2,1)S(1)} %bitcast.47), channel_id=1, replica_groups=mesh['tile'=8,'col'=4] {'col'}, dimensions={0} | all-to-all | bytes 2097152 | tf_op jit(solution)/shard_map/all_to_all | solution.py:296
  128.1 0.7 copy.44
  128.8 1.5 reshape.142.x_ref
  130.3 59.9 %shard_map.69 = bf16[4,2048,256]{2,1,0:T(8,128)(2,1)} custom-call(bf16[2,2048,4096]{2,1,0:T(8,128)(2,1)} %z_ref.3, bf16[512,1024]{1,0:T(8,128)(2,1)} %reshape.142.x_ref), custom_call_target="tpu_custom_call" | custom-call | tf_op jit(solution)/shard_map/pallas_call | solution.py:228
  191.5 75.3 %reduce-scatter.3.cloned.1.call-done = bf16[1,2048,256]{2,1,0:T(8,128)(2,1)} async-done(((bf16[4,2048,256]{2,1,0:T(8,128)(2,1)}), bf16[1,2048,256]{2,1,0:T(8,128)(2,1)}) %reduce-scatter.3.cloned.1.call-update) | async-done | bytes 1048592 | tf_op jit(solution)/shard_map/reduce_scatter | solution.py:299
  266.8 1.3 reshape.143.x_ref
  268.1 52.0 %shard_map.70 = bf16[2048,2,128]{2,1,0:T(2,128)(2,1)S(1)} custom-call(s32[2048]{0:T(1024)S(1)} %reshape.137.index_ref, bf16[2048,2,128]{2,1,0:T(2,128)(2,1)S(1)} %reshape.143.x_ref), custom_call_target="tpu_custom_call" | custom-call | tf_op jit(solution)/shard_map/pallas_call | solution.py:166
  320.4 1.4 fusion.5
  321.7 0.7 convolution_convert_fusion.1
  322.5 52.0 %shard_map.71 = bf16[2048,2,128]{2,1,0:T(2,128)(2,1)S(1)} custom-call(s32[2048]{0:T(1024)S(1)} %bitcast.49, bf16[2048,2,128]{2,1,0:T(2,128)(2,1)S(1)} %bitcast.42), custom_call_target="tpu_custom_call" | custom-call | tf_op jit(solution)/shard_map/pallas_call | solution.py:166
  374.5 30.6 %all_to_all.11 = bf16[4,512,2,128]{3,2,1,0:T(2,128)(2,1)S(1)} all-to-all(bf16[4,512,2,128]{3,2,1,0:T(2,128)(2,1)S(1)} %bitcast.46), channel_id=1, replica_groups=mesh['tile'=8,'col'=4] {'col'}, dimensions={0} | all-to-all | bytes 2097152 | tf_op jit(solution)/shard_map/all_to_all | solution.py:296
  405.8 1.5 reshape.146.x_ref
  407.3 59.8 %shard_map.72 = bf16[4,2048,256]{2,1,0:T(8,128)(2,1)} custom-call(bf16[2,2048,4096]{2,1,0:T(8,128)(2,1)} %z_ref.3, bf16[512,1024]{1,0:T(8,128)(2,1)} %reshape.146.x_ref), custom_call_target="tpu_custom_call" | custom-call | tf_op jit(solution)/shard_map/pallas_call | solution.py:228
  467.1 76.6 %reduce-scatter.5.cloned.1.call-done = bf16[1,2048,256]{2,1,0:T(8,128)(2,1)} async-done(((bf16[4,2048,256]{2,1,0:T(8,128)(2,1)}), bf16[1,2048,256]{2,1,0:T(8,128)(2,1)}) %reduce-scatter.5.cloned.1.call-update) | async-done | bytes 1048592 | tf_op jit(solution)/shard_map/reduce_scatter | solution.py:299
  543.7 1.3 reshape.147.x_ref
  545.1 52.0 %shard_map.73 = bf16[2048,2,128]{2,1,0:T(2,128)(2,1)S(1)} custom-call(s32[2048]{0:T(1024)S(1)} %reshape.137.index_ref, bf16[2048,2,128]{2,1,0:T(2,128)(2,1)S(1)} %reshape.147.x_ref), custom_call_target="tpu_custom_call" | custom-call | tf_op jit(solution)/shard_map/pallas_call | solution.py:166
  597.3 1.4 fusion.6
  598.7 0.7 convolution_convert_fusion
  599.7 1.7 copy.53
  601.3 3.7 copy.54
  (31 shorter events, 4.9 us)
Async XLA Ops:
  7.2 259.6 %reduce-scatter.3.cloned.1.call-start = ((), (), s32[]{:S(2)}) async-start(), calls=%async_computation.4 | async-start | bytes 5242880 | tf_op jit(solution)/shard_map/reduce_scatter | solution.py:299
  29.1 1.3 copy-start
  39.4 4.1 copy-start.1
  190.2 0.7 copy-start.2
  190.3 353.5 %reduce-scatter.5.cloned.1.call-start = ((), (), s32[]{:S(2)}) async-start(), calls=%async_computation.5 | async-start | bytes 5242880 | tf_op jit(solution)/shard_map/reduce_scatter | solution.py:299
Sparse Core Ops, SparseCore 0:
  190.4 76.3 reduce-scatter.2
  467.2 76.4 reduce-scatter.4

commit v3 on v2

--- a/solution.py
+++ b/solution.py
@@ -79,13 +79,13 @@
     def own(h):
         return x_ref.at[pl.ds(h * half, half)]
 
+    for h in (0, 1):
+        send(own(h), piece(0, 0, h, core), partner, 1, 0, 0, h)
     for h in (1, 0):
         send(own(h), piece(0, 0, h, core), device_at(0, 1), 0, 0, 1, h)
     for h in (0, 1):
         for o in others:
             send(own(h), piece(0, 0, h, core), device_at(o, 0), 0, (a_size - o) % a_size, 0, h)
-    for h in (0, 1):
-        send(own(h), piece(0, 0, h, core), partner, 1, 0, 0, h)
     local = pltpu.make_async_copy(
         x_ref, buf.at[chip_at(0, 0), pl.ds(pl.multiple_of(core * rows, rows), rows)], own_sem.at[0]
     )

time: 612 us -> 612 us (level)
  no operation moved by 1% of the time
where the time goes in v3:
time: 612 us
  Pallas kernels  327 us (53%)
  waiting for transfers between devices  152 us (25%)
  blocking collectives  71.1 us (12%)
  local copies, waits for them, and re-layouts  31.2 us (5%)
  between operations  15 us (2%)
  other arithmetic  12.3 us (2%)
    pallas_call x4, Pallas kernels, gather_and_pick(): pl.pallas_call(functools.partial(pick_kernel, tiles), out_shape=jax.Shape...  207 us
    reduce_scatter x2, waiting for transfers between devices, per_device(): summed = lax.psum_scatter(partial, 'col', scatter_dimension=0, tiled=True)  152 us
    pallas_call x2, Pallas kernels, gather_and_multiply(): pl.pallas_call(functools.partial(product_kernel, tiles), out_shape=jax.Sh...  120 us
    all_to_all x2, blocking collectives, per_device(): lax.all_to_all(picked, 'col', split_axis=0, concat_axis=0, tiled=True)  61.6 us
  transfers between devices with their start and end apart: 2, of which 2 were waited for; matrix products, arithmetic and copies ran while one was open for 0% of the time, Pallas kernels for 0%

profile of v3, /device:TPU:0, one launch (start us, length us, event | category | flops | bytes accessed | tf_op | source)
XLA Modules:
  0.0 612.0 jit_solution(3931978882087323477)
XLA Ops:
  7.2 0.9 reshape.136
  8.2 1.2 dynamic-slice
  10.1 0.9 dynamic-update-slice
  10.9 9.5 %all-reduce = s32[256]{0:T(256)S(1)} all-reduce(s32[256]{0:T(256)S(1)} %dynamic-update-slice), channel_id=1, replica_groups=mesh['tile'=8,'col'=4] {'tile'}, use_global_device_ids=true, to_apply=%add | all-reduce | flops 256 | bytes 2048
  20.4 0.7 gather_fusion.1
  21.3 7.8 %select_convert_fusion.1 = (bf16[16384,128]{1,0:T(8,128)(2,1)S(1)}, bf16[16384,128]{1,0:T(8,128)(2,1)S(1)}) fusion(s32[16384]{0:T(1024)S(1)} %get-tuple-element.20, s32[16384]{0:T(1024)S(1)} %get-tuple-element.16, s32[16384]{0:T(1024)S(1)} %get-tuple-element.19), kind=kLoop, calls=%fused_computation.7 | loop fusion | flops 10485760 | bytes 8585216 | tf_op jit(solution)/shard_map/convert_element_type | solution.py:253
  29.1 1.3 fusion
  31.7 7.7 %copy.39 = bf16[32,64,2,64,2]{0,4,3,2,1:T(2,128)(2,1)} copy(bf16[32,64,2,64,2]{3,1,0,4,2:T(8,128)(2,1)S(1)} %pad_maximum_fusion) | data formatting | bytes 2097152 | tf_op jit(solution)/shard_map/stack | solution.py:282
  39.4 4.1 copy.50
  43.5 1.0 copy.40
  45.2 0.8 convolution_convert_fusion.2
  45.9 51.1 %shard_map.68 = bf16[2048,2,128]{2,1,0:T(2,128)(2,1)S(1)} custom-call(s32[2048]{0:T(1024)S(1)} %bitcast.48, bf16[2048,2,128]{2,1,0:T(2,128)(2,1)S(1)} %bitcast.45), custom_call_target="tpu_custom_call" | custom-call | tf_op jit(solution)/shard_map/pallas_call | solution.py:166
  97.1 31.0 %all_to_all.10 = bf16[4,512,2,128]{3,2,1,0:T(2,128)(2,1)S(1)} all-to-all(bf16[4,512,2,128]{3,2,1,0:T(2,128)(2,1)S(1)} %bitcast.47), channel_id=1, replica_groups=mesh['tile'=8,'col'=4] {'col'}, dimensions={0} | all-to-all | bytes 2097152 | tf_op jit(solution)/shard_map/all_to_all | solution.py:296
  128.1 0.7 copy.44
  128.8 1.5 reshape.142.x_ref
  130.4 59.9 %shard_map.69 = bf16[4,2048,256]{2,1,0:T(8,128)(2,1)} custom-call(bf16[2,2048,4096]{2,1,0:T(8,128)(2,1)} %z_ref.3, bf16[512,1024]{1,0:T(8,128)(2,1)} %reshape.142.x_ref), custom_call_target="tpu_custom_call" | custom-call | tf_op jit(solution)/shard_map/pallas_call | solution.py:228
  191.5 75.3 %reduce-scatter.3.cloned.1.call-done = bf16[1,2048,256]{2,1,0:T(8,128)(2,1)} async-done(((bf16[4,2048,256]{2,1,0:T(8,128)(2,1)}), bf16[1,2048,256]{2,1,0:T(8,128)(2,1)}) %reduce-scatter.3.cloned.1.call-update) | async-done | bytes 1048592 | tf_op jit(solution)/shard_map/reduce_scatter | solution.py:299
  266.8 1.3 reshape.143.x_ref
  268.1 52.0 %shard_map.70 = bf16[2048,2,128]{2,1,0:T(2,128)(2,1)S(1)} custom-call(s32[2048]{0:T(1024)S(1)} %reshape.137.index_ref, bf16[2048,2,128]{2,1,0:T(2,128)(2,1)S(1)} %reshape.143.x_ref), custom_call_target="tpu_custom_call" | custom-call | tf_op jit(solution)/shard_map/pallas_call | solution.py:166
  320.4 1.4 fusion.5
  321.7 0.8 convolution_convert_fusion.1
  322.5 52.0 %shard_map.71 = bf16[2048,2,128]{2,1,0:T(2,128)(2,1)S(1)} custom-call(s32[2048]{0:T(1024)S(1)} %bitcast.49, bf16[2048,2,128]{2,1,0:T(2,128)(2,1)S(1)} %bitcast.42), custom_call_target="tpu_custom_call" | custom-call | tf_op jit(solution)/shard_map/pallas_call | solution.py:166
  374.5 30.6 %all_to_all.11 = bf16[4,512,2,128]{3,2,1,0:T(2,128)(2,1)S(1)} all-to-all(bf16[4,512,2,128]{3,2,1,0:T(2,128)(2,1)S(1)} %bitcast.46), channel_id=1, replica_groups=mesh['tile'=8,'col'=4] {'col'}, dimensions={0} | all-to-all | bytes 2097152 | tf_op jit(solution)/shard_map/all_to_all | solution.py:296
  405.8 1.5 reshape.146.x_ref
  407.3 59.8 %shard_map.72 = bf16[4,2048,256]{2,1,0:T(8,128)(2,1)} custom-call(bf16[2,2048,4096]{2,1,0:T(8,128)(2,1)} %z_ref.3, bf16[512,1024]{1,0:T(8,128)(2,1)} %reshape.146.x_ref), custom_call_target="tpu_custom_call" | custom-call | tf_op jit(solution)/shard_map/pallas_call | solution.py:228
  467.1 76.6 %reduce-scatter.5.cloned.1.call-done = bf16[1,2048,256]{2,1,0:T(8,128)(2,1)} async-done(((bf16[4,2048,256]{2,1,0:T(8,128)(2,1)}), bf16[1,2048,256]{2,1,0:T(8,128)(2,1)}) %reduce-scatter.5.cloned.1.call-update) | async-done | bytes 1048592 | tf_op jit(solution)/shard_map/reduce_scatter | solution.py:299
  543.7 1.3 reshape.147.x_ref
  545.1 52.0 %shard_map.73 = bf16[2048,2,128]{2,1,0:T(2,128)(2,1)S(1)} custom-call(s32[2048]{0:T(1024)S(1)} %reshape.137.index_ref, bf16[2048,2,128]{2,1,0:T(2,128)(2,1)S(1)} %reshape.147.x_ref), custom_call_target="tpu_custom_call" | custom-call | tf_op jit(solution)/shard_map/pallas_call | solution.py:166
  597.3 1.4 fusion.6
  598.7 0.8 convolution_convert_fusion
  599.7 1.7 copy.53
  601.4 3.7 copy.54
  (31 shorter events, 4.9 us)
Async XLA Ops:
  7.2 259.6 %reduce-scatter.3.cloned.1.call-start = ((), (), s32[]{:S(2)}) async-start(), calls=%async_computation.4 | async-start | bytes 5242880 | tf_op jit(solution)/shard_map/reduce_scatter | solution.py:299
  29.1 1.3 copy-start
  39.4 4.1 copy-start.1
  190.2 0.7 copy-start.2
  190.3 353.5 %reduce-scatter.5.cloned.1.call-start = ((), (), s32[]{:S(2)}) async-start(), calls=%async_computation.5 | async-start | bytes 5242880 | tf_op jit(solution)/shard_map/reduce_scatter | solution.py:299
Sparse Core Ops, SparseCore 0:
  190.4 76.3 reduce-scatter.2
  467.2 76.4 reduce-scatter.4
